TPU v7x, 32 devices: a whole 2x2x4 slice. The times are simulated.
32 devices in a mesh: row: 4 (over y, x), col: 8 (over z, core).
Axes of the slice: x: 2, y: 2, z: 4, core: 2. Of those that a mesh axis runs over, the one named last changes fastest.
Arguments:
- new_row: float32 [128, 96, 128], P('row', 'col'), may hold values from -4 to 4
- history: float32 [96, 96, 128, 128], P('row', 'col'), may hold values from -0.0546875 to 0.0546875
- hamiltonian: float32 [128, 128], replicated, may hold values from -0.5 to 0.5
Outputs:
- rows_out: float32 [3, 128, 96, 128], P(None, 'row', 'col')
All inputs are finite; a program needn't handle non-finite values.
Results may differ from a plain program's by a relative error of at most 0.00026.
Values sent between devices are 32-bit elements; how exact they have to be, the bound alone decides.
No kernel may reach another device: no remote copies, remote signals or barrier semaphores. Data moves between devices by JAX's collectives and lax.ppermute only.
A program may use at most 128 MiB of HBM per device.

v0:
```python
import jax
import jax.numpy as jnp
from jax import lax
from jax.sharding import PartitionSpec as P

STEPS = 3
time_step = 0.2


def sigma_panel(sigma_all, tile_rows):
    row_start = lax.axis_index("row") * tile_rows
    pieces = lax.all_to_all(sigma_all, "col", split_axis=0, concat_axis=1, tiled=True)
    needed = lax.dynamic_slice_in_dim(pieces, row_start, tile_rows, 1)
    return lax.all_gather(needed, "col", axis=0, tiled=True)


def contract(sigma_rows, history):
    return jnp.einsum(
        "isl,stlj->itj",
        sigma_rows,
        history,
        precision=lax.Precision.HIGHEST,
        preferred_element_type=jnp.float32,
    )


def advance(current, hamiltonian, collision):
    kinetic = jnp.einsum(
        "itl,lj->itj",
        current,
        hamiltonian,
        precision=lax.Precision.HIGHEST,
        preferred_element_type=jnp.float32,
    )
    return current - time_step * (kinetic + collision)


def per_device(new_row, history, hamiltonian):
    tile_rows = history.shape[0]
    results = []
    current = new_row
    for step_index in range(STEPS):
        sigma_local = current * current * current
        sigma_all = lax.all_gather(sigma_local, "row", axis=0, tiled=True)
        sigma_rows = sigma_panel(sigma_all, tile_rows)
        collision = lax.psum_scatter(
            contract(sigma_rows, history), "row", scatter_dimension=0, tiled=True
        )
        current = advance(current, hamiltonian, collision)
        results.append(current)
    return jnp.stack(results)


def solution(mesh):
    placed = (P("row", "col", None), P("row", "col", None, None), P())
    return jax.shard_map(
        per_device,
        mesh=mesh,
        in_specs=placed,
        out_specs=P(None, "row", "col", None),
        check_vma=False,
    )
```

profile of v0, /device:TPU:0, one launch (start us, length us, event | category | flops | bytes accessed | tf_op | source)
XLA Modules:
  0.0 342.0 jit_solution(1827196471069993955)
XLA Ops:
  6.5 0.0 copy-start
  6.5 1.0 multiply_multiply_fusion.2
  7.5 12.7 %all_gather.18 = f32[128,12,128]{2,0,1:T(8,128)S(1)} all-gather(f32[32,12,128]{2,0,1:T(8,128)S(1)} %multiply_multiply_fusion.2), channel_id=1, replica_groups=mesh['row'=4,'col'=8] {'row'}, dimensions={0}, use_global_device_ids=true | all-gather | bytes 983040 | tf_op jit(solution)/shard_map/all_gather | solution.py:44
  20.2 1.5 copy.21
  21.6 4.9 %all-to-all-start = ((f32[128,12,128]{2,1,0:T(8,128)}), f32[128,12,128]{2,1,0:T(8,128)S(1)}, u32[]{:S(2)}, u32[]{:S(2)}) async-start(f32[128,12,128]{2,1,0:T(8,128)} %copy.21), calls=%async_computation | async-start | bytes 2097152 | tf_op jit(solution)/shard_map/all_to_all | solution.py:12
  26.5 0.0 all-gather.4.cloned.1.call-start
  26.6 26.5 %all-to-all-done = f32[128,12,128]{2,1,0:T(8,128)S(1)} async-done(((f32[128,12,128]{2,1,0:T(8,128)}), f32[128,12,128]{2,1,0:T(8,128)S(1)}, u32[]{:S(2)}, u32[]{:S(2)}) %all-to-all-start) | async-done | bytes 786464 | tf_op jit(solution)/shard_map/all_to_all | solution.py:12
  53.1 0.2 copy.22
  53.3 0.7 constant_dynamic-slice_fusion.2
  54.0 0.0 all-gather.4.cloned.1.call-update
  54.1 0.0 copy-start.1
  54.1 0.0 reduce-scatter.4.cloned.1.call-start
  54.1 23.3 %all-gather.4.cloned.1.call-done = f32[128,24,128]{2,0,1:T(8,128)} async-done(((f32[16,24,128]{2,0,1:T(8,128)}), f32[128,24,128]{2,0,1:T(8,128)}) %all-gather.4.cloned.1.call-update) | async-done | bytes 1572880 | tf_op jit(solution)/shard_map/all_gather | solution.py:14
  77.5 14.3 %fusion.6 = f32[128,12,128]{2,0,1:T(8,128)} fusion(f32[24,12,128,128]{3,2,1,0:T(8,128)} %param.4, f32[128,24,128]{2,0,1:T(8,128)} %all-gather.4.cloned.1.call-done), kind=kOutput, calls=%fused_computation.6 | convolution fusion | flops 7247757312 | bytes 21233664 | tf_op jit(solution)/shard_map/isl,stlj->itj/dot_general | solution.py:18
  91.7 0.0 reduce-scatter.4.cloned.1.call-update
  91.7 0.0 all-gather.6.cloned.1.call-start
  91.8 25.4 %reduce-scatter.4.cloned.1.call-done = f32[32,12,128]{2,0,1:T(8,128)} async-done(((f32[128,12,128]{2,0,1:T(8,128)}), f32[32,12,128]{2,0,1:T(8,128)}) %reduce-scatter.4.cloned.1.call-update) | async-done | bytes 196624 | tf_op jit(solution)/shard_map/reduce_scatter | solution.py:46
  117.2 0.0 copy-done
  117.2 0.0 copy-done.1
  117.2 1.2 multiply_multiply_fusion.1
  118.4 11.2 %all_gather.20 = f32[128,12,128]{2,0,1:T(8,128)S(1)} all-gather(f32[32,12,128]{2,0,1:T(8,128)S(1)} %get-tuple-element.5), channel_id=1, replica_groups=mesh['row'=4,'col'=8] {'row'}, dimensions={0}, use_global_device_ids=true | all-gather | bytes 983040 | tf_op jit(solution)/shard_map/all_gather | solution.py:44
  129.6 0.5 copy.24
  130.1 31.0 %all_to_all.54 = f32[128,12,128]{2,1,0:T(8,128)S(1)} all-to-all(f32[128,12,128]{2,1,0:T(8,128)S(1)} %copy.24), channel_id=1, replica_groups=mesh['row'=4,'col'=8] {'col'}, dimensions={0} | all-to-all | bytes 1572864 | tf_op jit(solution)/shard_map/all_to_all | solution.py:12
  161.0 0.2 copy.25
  161.3 0.7 constant_dynamic-slice_fusion.1
  162.0 0.0 all-gather.6.cloned.1.call-update
  162.0 0.0 reduce-scatter.6.cloned.1.call-start
  162.0 23.3 %all-gather.6.cloned.1.call-done = f32[128,24,128]{2,0,1:T(8,128)} async-done(((f32[16,24,128]{2,0,1:T(8,128)}), f32[128,24,128]{2,0,1:T(8,128)}) %all-gather.6.cloned.1.call-update) | async-done | bytes 1572880 | tf_op jit(solution)/shard_map/all_gather | solution.py:14
  185.4 14.3 %fusion.9 = f32[128,12,128]{2,0,1:T(8,128)} fusion(f32[24,12,128,128]{3,2,1,0:T(8,128)} %param.4, f32[128,24,128]{2,0,1:T(8,128)} %all-gather.6.cloned.1.call-done), kind=kOutput, calls=%fused_computation.7 | convolution fusion | flops 7247757312 | bytes 21233664 | tf_op jit(solution)/shard_map/isl,stlj->itj/dot_general | solution.py:18
  199.6 0.0 reduce-scatter.6.cloned.1.call-update
  199.6 0.0 all-gather.8.cloned.1.call-start
  199.7 25.4 %reduce-scatter.6.cloned.1.call-done = f32[32,12,128]{2,0,1:T(8,128)} async-done(((f32[128,12,128]{2,0,1:T(8,128)}), f32[32,12,128]{2,0,1:T(8,128)}) %reduce-scatter.6.cloned.1.call-update) | async-done | bytes 196624 | tf_op jit(solution)/shard_map/reduce_scatter | solution.py:46
  225.1 1.2 multiply_multiply_fusion
  226.3 11.2 %all_gather.22 = f32[128,12,128]{2,0,1:T(8,128)S(1)} all-gather(f32[32,12,128]{2,0,1:T(8,128)S(1)} %get-tuple-element.7), channel_id=1, replica_groups=mesh['row'=4,'col'=8] {'row'}, dimensions={0}, use_global_device_ids=true | all-gather | bytes 983040 | tf_op jit(solution)/shard_map/all_gather | solution.py:44
  237.5 0.5 copy.27
  238.0 31.0 %all_to_all.55 = f32[128,12,128]{2,1,0:T(8,128)S(1)} all-to-all(f32[128,12,128]{2,1,0:T(8,128)S(1)} %copy.27), channel_id=1, replica_groups=mesh['row'=4,'col'=8] {'col'}, dimensions={0} | all-to-all | bytes 1572864 | tf_op jit(solution)/shard_map/all_to_all | solution.py:12
  268.9 0.2 copy.28
  269.2 0.7 constant_dynamic-slice_fusion
  269.9 0.0 all-gather.8.cloned.1.call-update
  269.9 0.2 reduce-scatter.8.cloned.1.call-start
  270.1 23.1 %all-gather.8.cloned.1.call-done = f32[128,24,128]{2,0,1:T(8,128)} async-done(((f32[16,24,128]{2,0,1:T(8,128)}), f32[128,24,128]{2,0,1:T(8,128)}) %all-gather.8.cloned.1.call-update) | async-done | bytes 1572880 | tf_op jit(solution)/shard_map/all_gather | solution.py:14
  293.3 14.3 %fusion.12 = f32[128,12,128]{2,0,1:T(8,128)} fusion(f32[24,12,128,128]{3,2,1,0:T(8,128)} %param.4, f32[128,24,128]{2,0,1:T(8,128)} %all-gather.8.cloned.1.call-done), kind=kOutput, calls=%fused_computation.8 | convolution fusion | flops 7247757312 | bytes 21233664 | tf_op jit(solution)/shard_map/isl,stlj->itj/dot_general | solution.py:18
  307.5 0.0 reduce-scatter.8.cloned.1.call-update
  307.6 25.4 %reduce-scatter.8.cloned.1.call-done = f32[32,12,128]{2,0,1:T(8,128)} async-done(((f32[128,12,128]{2,0,1:T(8,128)}), f32[32,12,128]{2,0,1:T(8,128)}) %reduce-scatter.8.cloned.1.call-update) | async-done | bytes 196624 | tf_op jit(solution)/shard_map/reduce_scatter | solution.py:46
  333.0 1.2 fusion.17
  334.2 0.9 pad_maximum_fusion
Async XLA Ops:
  6.5 110.6 %copy-start = (f32[128,128]{1,0:T(8,128)S(1)}, f32[128,128]{1,0:T(8,128)}, u32[]{:S(2)}) copy-start(f32[128,128]{1,0:T(8,128)} %param.5) | copy-start | bytes 196612
  21.6 31.4 %all-to-all-start = ((f32[128,12,128]{2,1,0:T(8,128)}), f32[128,12,128]{2,1,0:T(8,128)S(1)}, u32[]{:S(2)}, u32[]{:S(2)}) async-start(f32[128,12,128]{2,1,0:T(8,128)} %copy.21), calls=%async_computation | async-start | bytes 2097152 | tf_op jit(solution)/shard_map/all_to_all | solution.py:12
  26.5 50.9 %all-gather.4.cloned.1.call-start = ((), (), s32[]{:S(2)}) async-start(), calls=%async_computation.6 | async-start | bytes 1769472 | tf_op jit(solution)/shard_map/all_gather | solution.py:14
  54.1 63.1 %copy-start.1 = (f32[32,12,128]{2,0,1:T(8,128)S(1)}, f32[32,12,128]{2,0,1:T(8,128)}, u32[]{:S(2)}) copy-start(f32[32,12,128]{2,0,1:T(8,128)} %param.3) | copy-start | bytes 589828
  54.1 63.1 %reduce-scatter.4.cloned.1.call-start = ((), (), s32[]{:S(2)}) async-start(), calls=%async_computation.7 | async-start | bytes 983040 | tf_op jit(solution)/shard_map/reduce_scatter | solution.py:46
  91.7 93.6 %all-gather.6.cloned.1.call-start = ((), (), s32[]{:S(2)}) async-start(), calls=%async_computation.8 | async-start | bytes 1769472 | tf_op jit(solution)/shard_map/all_gather | solution.py:14
  162.0 63.1 %reduce-scatter.6.cloned.1.call-start = ((), (), s32[]{:S(2)}) async-start(), calls=%async_computation.9 | async-start | bytes 983040 | tf_op jit(solution)/shard_map/reduce_scatter | solution.py:46
  199.6 93.6 %all-gather.8.cloned.1.call-start = ((), (), s32[]{:S(2)}) async-start(), calls=%async_computation.10 | async-start | bytes 1769472 | tf_op jit(solution)/shard_map/all_gather | solution.py:14
  269.9 63.1 %reduce-scatter.8.cloned.1.call-start = ((), (), s32[]{:S(2)}) async-start(), calls=%async_computation.11 | async-start | bytes 983040 | tf_op jit(solution)/shard_map/reduce_scatter | solution.py:46
Sparse Core Ops, SparseCore 0:
  54.2 23.2 all-gather.3
  91.9 25.2 reduce-scatter.3
  162.1 23.2 all-gather.5
  199.8 25.2 reduce-scatter.5
  270.0 23.2 all-gather.7
  307.7 25.2 reduce-scatter.7
where the time goes:
time: 342 us
  waiting for transfers between devices  173 us (51%)
  blocking collectives  96.9 us (28%)
  matrix products  46.5 us (14%)
  between operations  13.5 us (4%)
  starting transfers between devices  5.3 us (2%)
  local copies, waits for them, and re-layouts  5.23 us (2%)
    reduce_scatter x3, waiting for transfers between devices, per_device(): lax.psum_scatter(contract(sigma_rows, history), 'row', scatter_dimension=...  76.2 us
    all_gather x3, waiting for transfers between devices, sigma_panel(): return lax.all_gather(needed, 'col', axis=0, tiled=True)  69.8 us
    all_to_all x2, blocking collectives, sigma_panel(): lax.all_to_all(sigma_all, 'col', split_axis=0, concat_axis=1, tiled=True)  61.9 us
    dot_general x3, matrix products, contract(): jnp.einsum('isl,stlj->itj', sigma_rows, history, precision=lax.Precision....  42.8 us
    all_gather x3, blocking collectives, per_device(): sigma_all = lax.all_gather(sigma_local, 'row', axis=0, tiled=True)  35 us
    all_to_all x1, waiting for transfers between devices, sigma_panel(): lax.all_to_all(sigma_all, 'col', split_axis=0, concat_axis=1, tiled=True)  26.5 us
  transfers between devices with their start and end apart: 7, of which 7 were waited for; matrix products, arithmetic and copies ran while one was open for 0% of the time, Pallas kernels for 0%

commit v1 on v0

--- a/solution.py
+++ b/solution.py
@@ -9,7 +9,10 @@
 
 def sigma_panel(sigma_all, tile_rows):
     row_start = lax.axis_index("row") * tile_rows
-    pieces = lax.all_to_all(sigma_all, "col", split_axis=0, concat_axis=1, tiled=True)
+    pieces = jnp.concatenate(
+        lax.all_to_all(jnp.stack(jnp.split(sigma_all, lax.axis_size("col"), axis=0)), "col", 0, 0),
+        axis=1,
+    )
     needed = lax.dynamic_slice_in_dim(pieces, row_start, tile_rows, 1)
     return lax.all_gather(needed, "col", axis=0, tiled=True)
 

time: 342 us -> 328 us (0.959)
  blocking collectives: 96.9 us -> 85.7 us
  waiting for transfers between devices: 173 us -> 167 us
    all_to_all x2, blocking collectives: 61.9 us -> 50.7 us  [sigma_panel(): lax.all_to_all(jnp.stack(jnp.split(sigma_all, lax.axis_size('col'), axis=...]
    all_to_all x1, waiting for transfers between devices: 26.5 us -> 20.9 us  [sigma_panel(): lax.all_to_all(jnp.stack(jnp.split(sigma_all, lax.axis_size('col'), axis=...]
    unnamed x4 -> x25, local copies, waits for them, and re-layouts: 0.01 us -> 4.62 us
where the time goes in v1:
time: 328 us; the launch traced here: 327 us
  waiting for transfers between devices  167 us (51%)
  blocking collectives  85.7 us (26%)
  matrix products  46.5 us (14%)
  between operations  13.7 us (4%)
  local copies, waits for them, and re-layouts  7.37 us (2%)
  starting transfers between devices  5.3 us (2%)
    reduce_scatter x3, waiting for transfers between devices, per_device(): lax.psum_scatter(contract(sigma_rows, history), 'row', scatter_dimension=...  76.2 us
    all_gather x3, waiting for transfers between devices, sigma_panel(): return lax.all_gather(needed, 'col', axis=0, tiled=True)  69.8 us
    all_to_all x2, blocking collectives, sigma_panel(): lax.all_to_all(jnp.stack(jnp.split(sigma_all, lax.axis_size('col'), axis=...  50.7 us
    dot_general x3, matrix products, contract(): jnp.einsum('isl,stlj->itj', sigma_rows, history, precision=lax.Precision....  42.8 us
    all_gather x3, blocking collectives, per_device(): sigma_all = lax.all_gather(sigma_local, 'row', axis=0, tiled=True)  35 us
    all_to_all x1, waiting for transfers between devices, sigma_panel(): lax.all_to_all(jnp.stack(jnp.split(sigma_all, lax.axis_size('col'), axis=...  20.9 us
  transfers between devices with their start and end apart: 7, of which 7 were waited for; matrix products, arithmetic and copies ran while one was open for 0% of the time, Pallas kernels for 0%

profile of v1, /device:TPU:0, one launch (start us, length us, event | category | flops | bytes accessed | tf_op | source)
XLA Modules:
  0.0 327.3 jit_solution(3410378541279731374)
XLA Ops:
  6.5 0.0 copy-start
  6.5 1.0 multiply_multiply_fusion.2
  7.5 12.7 %all_gather.18 = f32[128,12,128]{2,0,1:T(8,128)S(1)} all-gather(f32[32,12,128]{2,0,1:T(8,128)S(1)} %multiply_multiply_fusion.2), channel_id=1, replica_groups=mesh['row'=4,'col'=8] {'row'}, dimensions={0}, use_global_device_ids=true | all-gather | bytes 983040 | tf_op jit(solution)/shard_map/all_gather | solution.py:47
  20.2 0.6 fusion.45
  20.8 0.6 fusion.44
  21.5 0.6 fusion.43
  22.1 0.6 fusion.42
  22.8 0.6 fusion.41
  23.4 0.6 fusion.40
  24.0 0.6 fusion.39
  24.7 0.7 fusion.38
  25.3 4.9 %all-to-all-start = ((f32[8,16,12,128]{3,1,2,0:T(8,128)}), f32[8,16,12,128]{3,1,2,0:T(8,128)S(1)}, u32[]{:S(2)}, u32[]{:S(2)}) async-start(f32[8,16,12,128]{3,1,2,0:T(8,128)} %fusion.38), calls=%async_computation | async-start | bytes 1572864 | tf_op jit(solution)/shard_map/all_to_all | solution.py:13
  30.2 0.0 all-gather.4.cloned.1.call-start
  30.3 20.9 %all-to-all-done = f32[8,16,12,128]{3,1,2,0:T(8,128)S(1)} async-done(((f32[8,16,12,128]{3,1,2,0:T(8,128)}), f32[8,16,12,128]{3,1,2,0:T(8,128)S(1)}, u32[]{:S(2)}, u32[]{:S(2)}) %all-to-all-start) | async-done | bytes 786464 | tf_op jit(solution)/shard_map/all_to_all | solution.py:13
  51.2 0.7 constant_dynamic-slice_fusion.2
  51.9 0.0 all-gather.4.cloned.1.call-update
  51.9 0.0 copy-start.1
  51.9 0.0 reduce-scatter.4.cloned.1.call-start
  51.9 23.3 %all-gather.4.cloned.1.call-done = f32[128,24,128]{2,0,1:T(8,128)} async-done(((f32[16,24,128]{2,0,1:T(8,128)}), f32[128,24,128]{2,0,1:T(8,128)}) %all-gather.4.cloned.1.call-update) | async-done | bytes 1572880 | tf_op jit(solution)/shard_map/all_gather | solution.py:17
  75.3 14.3 %fusion.6 = f32[128,12,128]{2,0,1:T(8,128)} fusion(f32[24,12,128,128]{3,2,1,0:T(8,128)} %param.4, f32[128,24,128]{2,0,1:T(8,128)} %all-gather.4.cloned.1.call-done), kind=kOutput, calls=%fused_computation.6 | convolution fusion | flops 7247757312 | bytes 21233664 | tf_op jit(solution)/shard_map/isl,stlj->itj/dot_general | solution.py:21
  89.5 0.0 reduce-scatter.4.cloned.1.call-update
  89.6 0.0 all-gather.6.cloned.1.call-start
  89.6 25.4 %reduce-scatter.4.cloned.1.call-done = f32[32,12,128]{2,0,1:T(8,128)} async-done(((f32[128,12,128]{2,0,1:T(8,128)}), f32[32,12,128]{2,0,1:T(8,128)}) %reduce-scatter.4.cloned.1.call-update) | async-done | bytes 196624 | tf_op jit(solution)/shard_map/reduce_scatter | solution.py:49
  115.0 0.0 copy-done
  115.0 0.0 copy-done.1
  115.0 1.2 multiply_multiply_fusion.1
  116.3 11.2 %all_gather.20 = f32[128,12,128]{2,0,1:T(8,128)S(1)} all-gather(f32[32,12,128]{2,0,1:T(8,128)S(1)} %get-tuple-element.5), channel_id=1, replica_groups=mesh['row'=4,'col'=8] {'row'}, dimensions={0}, use_global_device_ids=true | all-gather | bytes 983040 | tf_op jit(solution)/shard_map/all_gather | solution.py:47
  127.6 25.3 %all_to_all.15 = f32[8,16,12,128]{3,1,2,0:T(8,128)S(1)} all-to-all(f32[8,16,12,128]{3,1,2,0:T(8,128)S(1)} %fusion.30), channel_id=1, replica_groups=mesh['row'=4,'col'=8] {'col'}, dimensions={0} | all-to-all | bytes 1572864 | tf_op jit(solution)/shard_map/all_to_all | solution.py:13
  152.9 0.7 constant_dynamic-slice_fusion.1
  153.6 0.0 all-gather.6.cloned.1.call-update
  153.6 0.0 reduce-scatter.6.cloned.1.call-start
  153.7 23.3 %all-gather.6.cloned.1.call-done = f32[128,24,128]{2,0,1:T(8,128)} async-done(((f32[16,24,128]{2,0,1:T(8,128)}), f32[128,24,128]{2,0,1:T(8,128)}) %all-gather.6.cloned.1.call-update) | async-done | bytes 1572880 | tf_op jit(solution)/shard_map/all_gather | solution.py:17
  177.0 14.2 %fusion.9 = f32[128,12,128]{2,0,1:T(8,128)} fusion(f32[24,12,128,128]{3,2,1,0:T(8,128)} %param.4, f32[128,24,128]{2,0,1:T(8,128)} %all-gather.6.cloned.1.call-done), kind=kOutput, calls=%fused_computation.7 | convolution fusion | flops 7247757312 | bytes 21233664 | tf_op jit(solution)/shard_map/isl,stlj->itj/dot_general | solution.py:21
  191.2 0.0 reduce-scatter.6.cloned.1.call-update
  191.3 0.0 all-gather.8.cloned.1.call-start
  191.3 25.4 %reduce-scatter.6.cloned.1.call-done = f32[32,12,128]{2,0,1:T(8,128)} async-done(((f32[128,12,128]{2,0,1:T(8,128)}), f32[32,12,128]{2,0,1:T(8,128)}) %reduce-scatter.6.cloned.1.call-update) | async-done | bytes 196624 | tf_op jit(solution)/shard_map/reduce_scatter | solution.py:49
  216.7 1.2 multiply_multiply_fusion
  218.0 11.2 %all_gather.22 = f32[128,12,128]{2,0,1:T(8,128)S(1)} all-gather(f32[32,12,128]{2,0,1:T(8,128)S(1)} %get-tuple-element.7), channel_id=1, replica_groups=mesh['row'=4,'col'=8] {'row'}, dimensions={0}, use_global_device_ids=true | all-gather | bytes 983040 | tf_op jit(solution)/shard_map/all_gather | solution.py:47
  229.3 25.3 %all_to_all.16 = f32[8,16,12,128]{3,1,2,0:T(8,128)S(1)} all-to-all(f32[8,16,12,128]{3,1,2,0:T(8,128)S(1)} %fusion.22), channel_id=1, replica_groups=mesh['row'=4,'col'=8] {'col'}, dimensions={0} | all-to-all | bytes 1572864 | tf_op jit(solution)/shard_map/all_to_all | solution.py:13
  254.6 0.7 constant_dynamic-slice_fusion
  255.3 0.0 all-gather.8.cloned.1.call-update
  255.3 0.2 reduce-scatter.8.cloned.1.call-start
  255.5 23.1 %all-gather.8.cloned.1.call-done = f32[128,24,128]{2,0,1:T(8,128)} async-done(((f32[16,24,128]{2,0,1:T(8,128)}), f32[128,24,128]{2,0,1:T(8,128)}) %all-gather.8.cloned.1.call-update) | async-done | bytes 1572880 | tf_op jit(solution)/shard_map/all_gather | solution.py:17
  278.7 14.2 %fusion.12 = f32[128,12,128]{2,0,1:T(8,128)} fusion(f32[24,12,128,128]{3,2,1,0:T(8,128)} %param.4, f32[128,24,128]{2,0,1:T(8,128)} %all-gather.8.cloned.1.call-done), kind=kOutput, calls=%fused_computation.8 | convolution fusion | flops 7247757312 | bytes 21233664 | tf_op jit(solution)/shard_map/isl,stlj->itj/dot_general | solution.py:21
  292.9 0.0 reduce-scatter.8.cloned.1.call-update
  293.0 25.4 %reduce-scatter.8.cloned.1.call-done = f32[32,12,128]{2,0,1:T(8,128)} async-done(((f32[128,12,128]{2,0,1:T(8,128)}), f32[32,12,128]{2,0,1:T(8,128)}) %reduce-scatter.8.cloned.1.call-update) | async-done | bytes 196624 | tf_op jit(solution)/shard_map/reduce_scatter | solution.py:49
  318.4 1.2 fusion.17
  319.6 0.9 pad_maximum_fusion
  (16 shorter events, 0.1 us)
Async XLA Ops:
  6.5 108.5 %copy-start = (f32[128,128]{1,0:T(8,128)S(1)}, f32[128,128]{1,0:T(8,128)}, u32[]{:S(2)}) copy-start(f32[128,128]{1,0:T(8,128)} %param.5) | copy-start | bytes 196612
  25.3 25.8 %all-to-all-start = ((f32[8,16,12,128]{3,1,2,0:T(8,128)}), f32[8,16,12,128]{3,1,2,0:T(8,128)S(1)}, u32[]{:S(2)}, u32[]{:S(2)}) async-start(f32[8,16,12,128]{3,1,2,0:T(8,128)} %fusion.38), calls=%async_computation | async-start | bytes 1572864 | tf_op jit(solution)/shard_map/all_to_all | solution.py:13
  30.2 45.1 %all-gather.4.cloned.1.call-start = ((), (), s32[]{:S(2)}) async-start(), calls=%async_computation.6 | async-start | bytes 1769472 | tf_op jit(solution)/shard_map/all_gather | solution.py:17
  51.9 63.1 %copy-start.1 = (f32[32,12,128]{2,0,1:T(8,128)S(1)}, f32[32,12,128]{2,0,1:T(8,128)}, u32[]{:S(2)}) copy-start(f32[32,12,128]{2,0,1:T(8,128)} %param.3) | copy-start | bytes 589828
  51.9 63.1 %reduce-scatter.4.cloned.1.call-start = ((), (), s32[]{:S(2)}) async-start(), calls=%async_computation.7 | async-start | bytes 983040 | tf_op jit(solution)/shard_map/reduce_scatter | solution.py:49
  89.6 87.4 %all-gather.6.cloned.1.call-start = ((), (), s32[]{:S(2)}) async-start(), calls=%async_computation.8 | async-start | bytes 1769472 | tf_op jit(solution)/shard_map/all_gather | solution.py:17
  153.6 63.1 %reduce-scatter.6.cloned.1.call-start = ((), (), s32[]{:S(2)}) async-start(), calls=%async_computation.9 | async-start | bytes 983040 | tf_op jit(solution)/shard_map/reduce_scatter | solution.py:49
  191.3 87.4 %all-gather.8.cloned.1.call-start = ((), (), s32[]{:S(2)}) async-start(), calls=%async_computation.10 | async-start | bytes 1769472 | tf_op jit(solution)/shard_map/all_gather | solution.py:17
  255.3 63.1 %reduce-scatter.8.cloned.1.call-start = ((), (), s32[]{:S(2)}) async-start(), calls=%async_computation.11 | async-start | bytes 983040 | tf_op jit(solution)/shard_map/reduce_scatter | solution.py:49
Sparse Core Ops, SparseCore 0:
  52.0 23.2 all-gather.3
  89.7 25.2 reduce-scatter.3
  153.7 23.2 all-gather.5
  191.4 25.2 reduce-scatter.5
  255.4 23.2 all-gather.7
  293.1 25.2 reduce-scatter.7
